TPU v7x, 32 devices: a whole 2x2x4 slice. The times are simulated.
32 devices in a mesh: groups: 2 (over y), branch: 2 (over core), tok: 8 (over z, x).
Axes of the slice: x: 2, y: 2, z: 4, core: 2. Of those that a mesh axis runs over, the one named last changes fastest.
Arguments:
- queries: bfloat16 [512, 4096], P(('groups', 'tok')), parts along dimension 0, may hold values from -8 to 8
- keys: bfloat16 [512, 4096], P(('groups', 'tok')), parts along dimension 0, may hold values from -8 to 8
- values: bfloat16 [512, 4096], P(('groups', 'tok')), parts along dimension 0, may hold values from -6 to 6
- keyboard: int32 [16], P('groups'), parts along dimension 0, may hold values from 0 to 15
- mouse: int32 [16], P('groups'), parts along dimension 0, may hold values from 0 to 31
- key_table: bfloat16 [16, 2, 4096], replicated, may hold values from -3 to 3
- mouse_table: bfloat16 [32, 2, 4096], replicated, may hold values from -3 to 3
- guidance: float32 [4], replicated, may hold values from 0.5 to 1.5
- out_weight: bfloat16 [4096, 64], replicated, may hold values from -0.09375 to 0.09375
- latent: float32 [512, 64], P(('groups', 'tok')), parts along dimension 0, may hold values from -6 to 6
- conv_in: bfloat16 [3, 3, 16, 384], replicated, may hold values from -0.5 to 0.5
- gain: float32 [384], replicated, may hold values from 0.5 to 1.5
- conv_out: bfloat16 [3, 3, 384, 3], replicated, may hold values from -0.109375 to 0.109375
Outputs:
- velocity: float32 [512, 64], P(('groups', 'tok')), parts along dimension 0
- frames_rgb: float32 [3, 32, 64], P(None, ('groups', 'tok')), parts along dimension 1
There are 2 independent parts, one for each index of `groups`. A program takes and returns all parts, laid end to end along the dimension named above; an argument that names none is the same for every part. Nothing has to cross between parts.
All inputs are finite; a program needn't handle non-finite values.
Results may differ from a plain program's by a relative error of at most 0.012.
Values may be sent and summed in bfloat16 or wider, within the bound.
A program may use at most 64 MiB of HBM per device.

v0:
```python
import jax
import jax.numpy as jnp
from jax import lax
from jax.sharding import PartitionSpec as P

HEAD_DIM = 128


step_size = 0.25
norm_eps = 1e-06


def passed_along(value, axis, steps):
    count = lax.axis_size(axis)
    pairs = [(source, (source + steps) % count) for source in range(count)]
    return lax.ppermute(value, axis, pairs)


def with_halo(block, sides, width):
    for axis, dim in sides:
        count = lax.axis_size(axis)
        forward = [(i, i + 1) for i in range(count - 1)]
        backward = [(target, source) for source, target in forward]
        low = lax.ppermute(
            lax.slice_in_dim(block, block.shape[dim] - width, None, axis=dim), axis, forward
        )
        high = lax.ppermute(lax.slice_in_dim(block, 0, width, axis=dim), axis, backward)
        block = jnp.concatenate([low, block, high], axis=dim)
    return block


def action_terms(keyboard, mouse, key_table, mouse_table, branch):
    flag_key = jnp.where(branch % 2 == 0, 1.0, 0.0).astype(jnp.float32)
    flag_mouse = jnp.where(branch < 2, 1.0, 0.0).astype(jnp.float32)
    pick_key = (
        keyboard[:, None] == jnp.arange(key_table.shape[0], dtype=jnp.int32)[None, :]
    ).astype(jnp.bfloat16)
    pick_mouse = (
        mouse[:, None] == jnp.arange(mouse_table.shape[0], dtype=jnp.int32)[None, :]
    ).astype(jnp.bfloat16)
    rows_key = jnp.einsum("fk,kcd->fcd", pick_key, key_table, preferred_element_type=jnp.float32)
    rows_mouse = jnp.einsum(
        "fk,kcd->fcd", pick_mouse, mouse_table, preferred_element_type=jnp.float32
    )
    return flag_key * rows_key + flag_mouse * rows_mouse


def pick_heads(array, first, taken, sets):
    lead = array.shape[:-1]
    split = array.reshape(lead + (sets, -1, HEAD_DIM))
    kept = lax.dynamic_slice_in_dim(split, first, taken, len(lead) + 1)
    return kept.reshape(lead + (sets * taken * HEAD_DIM,))


def heads_layout(array, rounds, sets):
    rows, width = array.shape
    piece = rows // rounds
    grouped = array.reshape(rounds, piece, sets, width // sets)
    return grouped.transpose(0, 2, 1, 3).reshape(rows * sets, width // sets)


def tokens_layout(array, rounds, sets):
    rows, width = array.shape
    piece = rows // (rounds * sets)
    grouped = array.reshape(rounds, sets, piece, width)
    return grouped.transpose(0, 2, 1, 3).reshape(rounds * piece, sets * width)


def attend(local_q, local_k, local_v, key_bias, value_term, rounds, sets):
    rows, width = local_q.shape
    heads_here = width // HEAD_DIM
    count_branches = key_bias.shape[0]
    frames = key_bias.shape[1]
    block = rows // frames
    scale = HEAD_DIM ** (-0.5)
    query = local_q.reshape(rows, heads_here, HEAD_DIM)
    bias_heads = key_bias.reshape(count_branches, frames, heads_here, HEAD_DIM)
    frame_scores = jnp.einsum(
        "qhd,bfhd->bhqf", query, bias_heads, preferred_element_type=jnp.float32
    )

    def visit(block_keys, block_values, carry):
        top, total, summed = carry
        base = jnp.einsum(
            "qhd,khd->hqk",
            query,
            block_keys.reshape(rows, heads_here, HEAD_DIM),
            preferred_element_type=jnp.float32,
        )
        grouped = base.reshape(heads_here, rows, frames, block)
        plain_values = block_values.astype(jnp.float32).reshape(frames, block, width)
        tops, totals, sums = ([], [], [])
        for which in range(count_branches):
            scores = (grouped + frame_scores[which][..., None]).reshape(
                heads_here, rows, rows
            ) * scale
            fresh = jnp.maximum(top[which], jnp.max(scores, axis=-1))
            shrink = jnp.exp(top[which] - fresh)
            raised = jnp.exp(scores - fresh[..., None])
            shifted = (plain_values + value_term[which][:, None, :]).astype(jnp.bfloat16)
            shifted = shifted.reshape(rows, heads_here, HEAD_DIM)
            product = jnp.einsum(
                "hqk,khd->hqd",
                raised.astype(jnp.bfloat16),
                shifted,
                preferred_element_type=jnp.float32,
            )
            tops.append(fresh)
            totals.append(total[which] * shrink + jnp.sum(raised, axis=-1))
            sums.append(summed[which] * shrink[..., None] + product)
        return (jnp.stack(tops), jnp.stack(totals), jnp.stack(sums))

    start = (
        jnp.full((count_branches, heads_here, rows), -jnp.inf, jnp.float32),
        jnp.zeros((count_branches, heads_here, rows), jnp.float32),
        jnp.zeros((count_branches, heads_here, rows, HEAD_DIM), jnp.float32),
    )
    carry = visit(local_k, local_v, start)

    def turn(step, state):
        block_keys, block_values, inner = state
        block_keys, block_values = passed_along((block_keys, block_values), "tok", sets)
        return (block_keys, block_values, visit(block_keys, block_values, inner))

    _, _, carry = lax.fori_loop(0, rounds - 1, turn, (local_k, local_v, carry))
    _, total, summed = carry
    attended = (summed / total[..., None]).astype(jnp.bfloat16)
    return attended.transpose(0, 2, 1, 3).reshape(count_branches, rows, heads_here * HEAD_DIM)


def clear_rows(array, depth, top_edge, bottom_edge):
    height = array.shape[0]
    place = jnp.arange(height, dtype=jnp.int32)
    drop = (place < depth) & top_edge | (place >= height - depth) & bottom_edge
    return jnp.where(drop[:, None, None], jnp.zeros_like(array), array)


def convolve(array, weight):
    rows = array.shape[0] - 2
    cols = array.shape[1]
    padded = jnp.pad(array, ((0, 0), (1, 1), (0, 0)))
    total = jnp.zeros((rows, cols, weight.shape[-1]), jnp.float32)
    for first in range(3):
        for second in range(3):
            window = padded[first : first + rows, second : second + cols, :]
            total = total + jnp.einsum(
                "rci,io->rco", window, weight[first, second], preferred_element_type=jnp.float32
            )
    return total


def normalize(features, gain):
    scaled = (
        features
        * lax.rsqrt(jnp.mean(features * features, axis=-1, keepdims=True) + norm_eps)
        * gain
    )
    return jax.nn.silu(scaled).astype(jnp.bfloat16)


def shards(
    queries,
    keys,
    values,
    keyboard,
    mouse,
    key_table,
    mouse_table,
    guidance,
    out_weight,
    latent,
    conv_in,
    gain,
    conv_out,
):
    count = lax.axis_size("tok")
    index = lax.axis_index("tok")
    branch = lax.axis_index("branch")
    sets = 8
    rounds = count // sets
    group = index % sets
    tok_dev, width = queries.shape
    per_group = width // (sets * HEAD_DIM)
    taken = per_group // 2
    first = branch * taken
    branches = [0, 1, 2, 3]
    spread_q = heads_layout(pick_heads(queries, first, taken, sets), rounds, sets)
    spread_k = heads_layout(pick_heads(keys, first, taken, sets), rounds, sets)
    spread_v = heads_layout(pick_heads(values, first, taken, sets), rounds, sets)
    local_q, local_k, local_v = (
        lax.all_to_all(spread_q, "tok", split_axis=0, concat_axis=0, tiled=True),
        lax.all_to_all(spread_k, "tok", split_axis=0, concat_axis=0, tiled=True),
        lax.all_to_all(spread_v, "tok", split_axis=0, concat_axis=0, tiled=True),
    )
    terms = jnp.stack(
        [action_terms(keyboard, mouse, key_table, mouse_table, which) for which in branches]
    )
    mine = pick_heads(terms, first, taken, sets)
    mine = mine.reshape(mine.shape[:-1] + (sets, -1))
    mine = lax.dynamic_index_in_dim(mine, group, 3, keepdims=False)
    key_bias = mine[:, :, 0].astype(jnp.bfloat16)
    value_term = mine[:, :, 1]
    outputs = attend(local_q, local_k, local_v, key_bias, value_term, rounds, sets)
    factors = [guidance[which] for which in branches]
    partial_value = factors[0] * outputs[0].astype(jnp.float32)
    for which in range(1, len(branches)):
        partial_value = partial_value + factors[which] * outputs[which].astype(jnp.float32)
    returned = lax.all_to_all(
        partial_value.astype(jnp.bfloat16), "tok", split_axis=0, concat_axis=0, tiled=True
    )
    split_weight = out_weight.reshape(sets, per_group, HEAD_DIM, -1)
    rows_weight = lax.dynamic_slice_in_dim(split_weight, first, taken, 1).reshape(
        sets * taken * HEAD_DIM, -1
    )
    projected = jnp.dot(
        tokens_layout(returned, rounds, sets), rows_weight, preferred_element_type=jnp.float32
    )
    velocity = lax.psum(projected, "branch")
    stepped = latent - step_size * velocity
    grid = (
        stepped.reshape(tok_dev, 2, 2, -1)
        .transpose(1, 0, 2, 3)
        .reshape(2, 2 * tok_dev, -1)
        .astype(jnp.bfloat16)
    )
    top_edge = index == 0
    bottom_edge = index == count - 1
    bordered = with_halo(grid, (("tok", 0),), 1)
    bordered = clear_rows(bordered, 1, top_edge, bottom_edge)
    hidden = normalize(convolve(bordered, conv_in), gain)
    hidden = with_halo(hidden, (("tok", 0),), 1)
    hidden = clear_rows(hidden, 1, top_edge, bottom_edge)
    colours = convolve(hidden, conv_out)
    return (velocity, colours.transpose(2, 0, 1))


def solution(mesh):
    placed = (
        P(("groups", "tok"), None),
        P(("groups", "tok"), None),
        P(("groups", "tok"), None),
        P("groups"),
        P("groups"),
        P(),
        P(),
        P(),
        P(),
        P(("groups", "tok"), None),
        P(),
        P(),
        P(),
    )
    return jax.shard_map(
        shards,
        mesh=mesh,
        in_specs=placed,
        out_specs=(P(("groups", "tok"), None), P(None, ("groups", "tok"), None)),
        check_vma=False,
    )
```

profile of v0, /device:TPU:8, one launch (start us, length us, event | category | flops | bytes accessed | tf_op | source)
XLA Modules:
  0.0 84.5 jit_solution(14081975832300911707)
XLA Ops:
  0.6 1.2 %reshape.276 = bf16[32,8,4,128]{3,2,1,0:T(4,128)(2,1)S(1)} reshape(bf16[32,4096]{1,0:T(8,128)(2,1)} %param.13) | data formatting | bytes 524288 | tf_op jit(solution)/shard_map/reshape | solution.py:50
  2.1 0.7 copy.132
  2.8 6.3 %all-to-all-start = ((bf16[8,32,256]{2,1,0:T(8,128)(2,1)}), bf16[8,32,256]{2,1,0:T(8,128)(2,1)S(1)}, u32[]{:S(2)}, u32[]{:S(2)}) async-start(bf16[8,32,256]{2,1,0:T(8,128)(2,1)} %bitcast.239), calls=%async_computation | async-start | bytes 262144 | tf_op jit(solution)/shard_map/all_to_all | solution.py:191
  9.0 0.7 copy-done.11
  9.7 0.4 fusion.43
  10.1 0.3 copy-done.12
  10.3 0.7 multiply_add_fusion
  11.1 0.2 copy.63
  11.3 0.2 copy.64
  11.6 0.8 copy-done.3
  12.4 0.2 reshape.280
  12.6 0.8 copy-done.4
  13.4 0.2 reshape.278
  13.7 0.3 constant_dynamic-slice_fusion.1
  14.0 0.4 copy-done.9
  14.3 0.6 fusion.135
  15.1 0.7 copy.131
  15.8 0.7 copy.130
  16.5 6.0 %all-to-all-start.1 = ((bf16[8,32,256]{2,1,0:T(8,128)(2,1)}), bf16[8,32,256]{2,1,0:T(8,128)(2,1)S(1)}, u32[]{:S(2)}, u32[]{:S(2)}) async-start(bf16[8,32,256]{2,1,0:T(8,128)(2,1)} %bitcast.238), calls=%async_computation.1 | async-start | bytes 262144 | tf_op jit(solution)/shard_map/all_to_all | solution.py:192
  22.7 5.0 %all-to-all-done.1 = bf16[8,32,256]{2,1,0:T(8,128)(2,1)S(1)} async-done(((bf16[8,32,256]{2,1,0:T(8,128)(2,1)}), bf16[8,32,256]{2,1,0:T(8,128)(2,1)S(1)}, u32[]{:S(2)}, u32[]{:S(2)}) %all-to-all-start.1) | async-done | bytes 131104 | tf_op jit(solution)/shard_map/all_to_all | solution.py:192
  27.7 5.4 %all-to-all-start.2 = ((bf16[8,32,256]{2,1,0:T(8,128)(2,1)}), bf16[8,32,256]{2,1,0:T(8,128)(2,1)S(1)}, u32[]{:S(2)}, u32[]{:S(2)}) async-start(bf16[8,32,256]{2,1,0:T(8,128)(2,1)} %bitcast.237), calls=%async_computation.2 | async-start | bytes 262144 | tf_op jit(solution)/shard_map/all_to_all | solution.py:193
  33.2 0.4 fusion.35
  33.6 0.5 fusion.27
  34.1 4.2 %all-to-all-done.2 = bf16[8,32,256]{2,1,0:T(8,128)(2,1)S(1)} async-done(((bf16[8,32,256]{2,1,0:T(8,128)(2,1)}), bf16[8,32,256]{2,1,0:T(8,128)(2,1)S(1)}, u32[]{:S(2)}, u32[]{:S(2)}) %all-to-all-start.2) | async-done | bytes 131104 | tf_op jit(solution)/shard_map/all_to_all | solution.py:193
  38.7 0.3 fusion
  38.9 0.3 fusion.1
  39.2 0.3 fusion.2
  39.5 0.3 fusion.3
  39.8 0.3 fusion.26
  40.2 2.6 %add_convert_fusion = bf16[1,256,2,128]{3,1,2,0:T(8,128)(2,1)S(1)} fusion(bf16[4,256,2,128]{3,1,2,0:T(8,128)(2,1)S(1)} %fusion.26, f32[]{:T(128)} %bitcast.41, f32[]{:T(128)} %bitcast.40, f32[]{:T(128)} %bitcast.39, f32[]{:T(128)} %bitcast), kind=kLoop, calls=%fused_computation.73 | loop fusion | flops 786432 | bytes 655376 | tf_op jit(solution)/shard_map/convert_element_type | solution.py:209
  42.9 0.7 reshape.290
  43.7 5.4 %all-to-all-start.3 = ((bf16[8,32,256]{2,1,0:T(8,128)(2,1)}), bf16[8,32,256]{2,1,0:T(8,128)(2,1)S(1)}, u32[]{:S(2)}, u32[]{:S(2)}) async-start(bf16[8,32,256]{2,1,0:T(8,128)(2,1)} %reshape.290), calls=%async_computation.3 | async-start | bytes 262144 | tf_op jit(solution)/shard_map/all_to_all | solution.py:208
  49.1 0.4 reshape.287
  49.5 0.3 constant_dynamic-slice_fusion
  49.8 0.2 reshape.288
  49.9 4.4 %all-to-all-done.3 = bf16[8,32,256]{2,1,0:T(8,128)(2,1)S(1)} async-done(((bf16[8,32,256]{2,1,0:T(8,128)(2,1)}), bf16[8,32,256]{2,1,0:T(8,128)(2,1)S(1)}, u32[]{:S(2)}, u32[]{:S(2)}) %all-to-all-start.3) | async-done | bytes 131104 | tf_op jit(solution)/shard_map/all_to_all | solution.py:208
  54.3 0.2 fusion.136
  54.5 3.5 %psum.7 = f32[32,64]{1,0:T(8,128)S(1)} all-reduce(f32[32,64]{1,0:T(8,128)S(1)} %fusion.136), channel_id=1, replica_groups=mesh['groups'=2,'branch'=2,'tok'=8] {'branch'}, use_global_device_ids=true, to_apply=%region_8.9 | all-reduce | flops 2048 | bytes 16384 | tf_op jit(solution)/shard_map/psum | solution.py:218
  58.1 0.6 copy-done.6
  58.9 3.7 %collective-permute-start.1 = (bf16[1,64,16]{1,2,0:T(8,128)(2,1)S(1)}, bf16[1,64,16]{1,2,0:T(8,128)(2,1)S(1)}, u32[]{:S(2)}, u32[]{:S(2)}) collective-permute-start(bf16[1,64,16]{1,2,0:T(8,128)(2,1)S(1)} %copy.85), channel_id=1, source_target_pairs={{1,0},{2,1},{3,2},{4,3},{5,4},{6,5},{7,6},{9,8},{10,9},{11,10},{12... | collective-permute-start | bytes 6152 | tf_op jit(solution)/shard_map/ppermute | solution.py:27
  62.8 2.1 %collective-permute-start = (bf16[1,64,16]{1,2,0:T(8,128)(2,1)S(1)}, bf16[1,64,16]{1,2,0:T(8,128)(2,1)S(1)}, u32[]{:S(2)}, u32[]{:S(2)}) collective-permute-start(bf16[1,64,16]{1,2,0:T(8,128)(2,1)S(1)} %copy.82), channel_id=1, source_target_pairs={{0,1},{1,2},{2,3},{3,4},{4,5},{5,6},{6,7},{8,9},{9,10},{10,11},{11... | collective-permute-start | bytes 6152 | tf_op jit(solution)/shard_map/ppermute | solution.py:24
  65.1 4.1 %collective-permute-done = bf16[1,64,16]{1,2,0:T(8,128)(2,1)S(1)} collective-permute-done((bf16[1,64,16]{1,2,0:T(8,128)(2,1)S(1)}, bf16[1,64,16]{1,2,0:T(8,128)(2,1)S(1)}, u32[]{:S(2)}, u32[]{:S(2)}) %collective-permute-start) | collective-permute-done | bytes 2080 | tf_op jit(solution)/shard_map/ppermute | solution.py:24
  69.3 0.3 fusion.61
  69.6 0.3 fusion.64
  69.9 0.3 fusion.66
  70.1 0.3 fusion.69
  70.4 0.3 fusion.71
  70.7 0.3 fusion.74
  71.0 0.2 fusion.8
  71.2 0.2 fusion.6
  71.4 0.3 multiply_reduce_fusion
  71.7 0.7 copy-done.10
  72.6 2.8 %collective-permute-start.3 = (bf16[1,64,384]{2,1,0:T(8,128)(2,1)S(1)}, bf16[1,64,384]{2,1,0:T(8,128)(2,1)S(1)}, u32[]{:S(2)}, u32[]{:S(2)}) collective-permute-start(bf16[1,64,384]{2,1,0:T(8,128)(2,1)S(1)} %get-tuple-element.29), channel_id=1, source_target_pairs={{1,0},{2,1},{3,2},{4,3},{5,4},{6,5},{7,6},{9,8},{10,9},{11,10},{12... | collective-permute-start | bytes 147464 | tf_op jit(solution)/shard_map/ppermute | solution.py:27
  75.4 3.0 %collective-permute-start.2 = (bf16[1,64,384]{2,1,0:T(8,128)(2,1)S(1)}, bf16[1,64,384]{2,1,0:T(8,128)(2,1)S(1)}, u32[]{:S(2)}, u32[]{:S(2)}) collective-permute-start(bf16[1,64,384]{2,1,0:T(8,128)(2,1)S(1)} %get-tuple-element.28), channel_id=1, source_target_pairs={{0,1},{1,2},{2,3},{3,4},{4,5},{5,6},{6,7},{8,9},{9,10},{10,11},{11... | collective-permute-start | bytes 147464 | tf_op jit(solution)/shard_map/ppermute | solution.py:24
  78.6 3.7 %collective-permute-done.2 = bf16[1,64,384]{2,1,0:T(8,128)(2,1)S(1)} collective-permute-done((bf16[1,64,384]{2,1,0:T(8,128)(2,1)S(1)}, bf16[1,64,384]{2,1,0:T(8,128)(2,1)S(1)}, u32[]{:S(2)}, u32[]{:S(2)}) %collective-permute-start.2) | collective-permute-done | bytes 49184 | tf_op jit(solution)/shard_map/ppermute | solution.py:24
  82.6 0.2 fusion.57
  82.7 0.2 fusion.56
  82.9 0.2 fusion.55
  83.1 0.2 fusion.54
  83.2 0.2 fusion.53
  83.4 0.2 fusion.14
  83.6 0.2 fusion.12
  83.7 0.2 fusion.10
  83.9 0.6 copy.87
  (64 shorter events, 2.8 us)
Async XLA Ops:
  0.6 9.4 %copy-start = (bf16[32,2,4096]{2,1,0:T(2,128)(2,1)S(1)}, bf16[32,2,4096]{2,1,0:T(2,128)(2,1)}, u32[]{:S(2)}) copy-start(bf16[32,2,4096]{2,1,0:T(2,128)(2,1)} %param.19) | copy-start | bytes 1572868
  2.1 6.9 %copy-start.2 = (bf16[16,2,4096]{2,1,0:T(2,128)(2,1)S(1)}, bf16[16,2,4096]{2,1,0:T(2,128)(2,1)}, u32[]{:S(2)}) copy-start(bf16[16,2,4096]{2,1,0:T(2,128)(2,1)} %param.18) | copy-start | bytes 786436
  2.8 13.8 %all-to-all-start = ((bf16[8,32,256]{2,1,0:T(8,128)(2,1)}), bf16[8,32,256]{2,1,0:T(8,128)(2,1)S(1)}, u32[]{:S(2)}, u32[]{:S(2)}) async-start(bf16[8,32,256]{2,1,0:T(8,128)(2,1)} %bitcast.239), calls=%async_computation | async-start | bytes 262144 | tf_op jit(solution)/shard_map/all_to_all | solution.py:191
  9.0 0.7 copy-start.11
  9.7 0.7 copy-start.12
  11.5 1.0 %copy-start.3 = (bf16[32,4096]{1,0:T(8,128)(2,1)S(1)}, bf16[32,4096]{1,0:T(8,128)(2,1)}, u32[]{:S(2)}) copy-start(bf16[32,4096]{1,0:T(8,128)(2,1)} %param.15) | copy-start | bytes 786436
  12.4 0.9 %copy-start.4 = (bf16[32,4096]{1,0:T(8,128)(2,1)S(1)}, bf16[32,4096]{1,0:T(8,128)(2,1)}, u32[]{:S(2)}) copy-start(bf16[32,4096]{1,0:T(8,128)(2,1)} %param.14) | copy-start | bytes 786436
  13.7 0.7 copy-start.9
  16.5 11.2 %all-to-all-start.1 = ((bf16[8,32,256]{2,1,0:T(8,128)(2,1)}), bf16[8,32,256]{2,1,0:T(8,128)(2,1)S(1)}, u32[]{:S(2)}, u32[]{:S(2)}) async-start(bf16[8,32,256]{2,1,0:T(8,128)(2,1)} %bitcast.238), calls=%async_computation.1 | async-start | bytes 262144 | tf_op jit(solution)/shard_map/all_to_all | solution.py:192
  27.7 10.7 %all-to-all-start.2 = ((bf16[8,32,256]{2,1,0:T(8,128)(2,1)}), bf16[8,32,256]{2,1,0:T(8,128)(2,1)S(1)}, u32[]{:S(2)}, u32[]{:S(2)}) async-start(bf16[8,32,256]{2,1,0:T(8,128)(2,1)} %bitcast.237), calls=%async_computation.2 | async-start | bytes 262144 | tf_op jit(solution)/shard_map/all_to_all | solution.py:193
  42.8 6.3 %copy-start.1 = (bf16[4096,64]{0,1:T(8,128)(2,1)S(1)}, bf16[4096,64]{0,1:T(8,128)(2,1)}, u32[]{:S(2)}) copy-start(bf16[4096,64]{0,1:T(8,128)(2,1)} %param.21) | copy-start | bytes 1572868
  43.7 10.7 %all-to-all-start.3 = ((bf16[8,32,256]{2,1,0:T(8,128)(2,1)}), bf16[8,32,256]{2,1,0:T(8,128)(2,1)S(1)}, u32[]{:S(2)}, u32[]{:S(2)}) async-start(bf16[8,32,256]{2,1,0:T(8,128)(2,1)} %reshape.290), calls=%async_computation.3 | async-start | bytes 262144 | tf_op jit(solution)/shard_map/all_to_all | solution.py:208
  54.5 3.5 %copy-start.8 = (f32[32,64]{1,0:T(8,128)S(1)}, f32[32,64]{1,0:T(8,128)}, u32[]{:S(2)}) copy-start(f32[32,64]{1,0:T(8,128)} %param.22) | copy-start | bytes 24580
  58.0 0.6 copy-start.6
  58.7 10.6 %copy-start.5 = (bf16[3,3,16,384]{3,2,1,0:T(8,128)(2,1)S(1)}, bf16[3,3,16,384]{3,2,1,0:T(8,128)(2,1)}, u32[]{:S(2)}) copy-start(bf16[3,3,16,384]{3,2,1,0:T(8,128)(2,1)} %param.23) | copy-start | bytes 331780
  58.9 6.2 %collective-permute-start.1 = (bf16[1,64,16]{1,2,0:T(8,128)(2,1)S(1)}, bf16[1,64,16]{1,2,0:T(8,128)(2,1)S(1)}, u32[]{:S(2)}, u32[]{:S(2)}) collective-permute-start(bf16[1,64,16]{1,2,0:T(8,128)(2,1)S(1)} %copy.85), channel_id=1, source_target_pairs={{1,0},{2,1},{3,2},{4,3},{5,4},{6,5},{7,6},{9,8},{10,9},{11,10},{12... | collective-permute-start | bytes 6152 | tf_op jit(solution)/shard_map/ppermute | solution.py:27
  62.8 6.4 %collective-permute-start = (bf16[1,64,16]{1,2,0:T(8,128)(2,1)S(1)}, bf16[1,64,16]{1,2,0:T(8,128)(2,1)S(1)}, u32[]{:S(2)}, u32[]{:S(2)}) collective-permute-start(bf16[1,64,16]{1,2,0:T(8,128)(2,1)S(1)} %copy.82), channel_id=1, source_target_pairs={{0,1},{1,2},{2,3},{3,4},{4,5},{5,6},{6,7},{8,9},{9,10},{10,11},{11... | collective-permute-start | bytes 6152 | tf_op jit(solution)/shard_map/ppermute | solution.py:24
  71.7 0.7 copy-start.10
  72.6 6.0 %collective-permute-start.3 = (bf16[1,64,384]{2,1,0:T(8,128)(2,1)S(1)}, bf16[1,64,384]{2,1,0:T(8,128)(2,1)S(1)}, u32[]{:S(2)}, u32[]{:S(2)}) collective-permute-start(bf16[1,64,384]{2,1,0:T(8,128)(2,1)S(1)} %get-tuple-element.29), channel_id=1, source_target_pairs={{1,0},{2,1},{3,2},{4,3},{5,4},{6,5},{7,6},{9,8},{10,9},{11,10},{12... | collective-permute-start | bytes 147464 | tf_op jit(solution)/shard_map/ppermute | solution.py:27
  75.4 7.0 %copy-start.7 = (bf16[3,3,384,3]{2,3,1,0:T(4,128)(2,1)S(1)}, bf16[3,3,384,3]{2,3,1,0:T(4,128)(2,1)}, u32[]{:S(2)}) copy-start(bf16[3,3,384,3]{2,3,1,0:T(4,128)(2,1)} %param.25) | copy-start | bytes 62212
  75.4 6.9 %collective-permute-start.2 = (bf16[1,64,384]{2,1,0:T(8,128)(2,1)S(1)}, bf16[1,64,384]{2,1,0:T(8,128)(2,1)S(1)}, u32[]{:S(2)}, u32[]{:S(2)}) collective-permute-start(bf16[1,64,384]{2,1,0:T(8,128)(2,1)S(1)} %get-tuple-element.28), channel_id=1, source_target_pairs={{0,1},{1,2},{2,3},{3,4},{4,5},{5,6},{6,7},{8,9},{9,10},{10,11},{11... | collective-permute-start | bytes 147464 | tf_op jit(solution)/shard_map/ppermute | solution.py:24
where the time goes:
time: 85.4 us; the launch traced here: 84.5 us
  starting transfers between devices  34.8 us (41%)
  waiting for transfers between devices  21.5 us (25%)
  local copies, waits for them, and re-layouts  12.8 us (15%)
  matrix products  6.85 us (8%)
  other arithmetic  3.91 us (5%)
  blocking collectives  3.49 us (4%)
  between operations  1.06 us (1%)
    ppermute x2, waiting for transfers between devices, with_halo(): lax.ppermute(lax.slice_in_dim(block, block.shape[dim] - width, None, axis...  7.82 us
    ppermute x2, starting transfers between devices, with_halo(): lax.ppermute(lax.slice_in_dim(block, 0, width, axis=dim), axis, backward)  6.55 us
    all_to_all x1, starting transfers between devices, shards(): lax.all_to_all(spread_q, 'tok', split_axis=0, concat_axis=0, tiled=True)  6.25 us
    all_to_all x1, starting transfers between devices, shards(): lax.all_to_all(spread_k, 'tok', split_axis=0, concat_axis=0, tiled=True)  6 us
    all_to_all x1, starting transfers between devices, shards(): lax.all_to_all(spread_v, 'tok', split_axis=0, concat_axis=0, tiled=True)  5.44 us
    all_to_all x1, starting transfers between devices, shards(): lax.all_to_all(partial_value.astype(jnp.bfloat16), 'tok', split_axis=0, c...  5.44 us
    ppermute x2, starting transfers between devices, with_halo(): lax.ppermute(lax.slice_in_dim(block, block.shape[dim] - width, None, axis...  5.14 us
    all_to_all x1, waiting for transfers between devices, shards(): lax.all_to_all(spread_k, 'tok', split_axis=0, concat_axis=0, tiled=True)  4.98 us
  transfers between devices with their start and end apart: 8, of which 6 were waited for; matrix products, arithmetic and copies ran while one was open for 8% of the time, Pallas kernels for 0%

commit v1 on v0

--- a/solution.py
+++ b/solution.py
@@ -1,7 +1,14 @@
+import functools
+import math
+
 import jax
 import jax.numpy as jnp
 from jax import lax
+from jax.experimental import pallas as pl
+from jax.experimental.pallas import tpu as pltpu
 from jax.sharding import PartitionSpec as P
+
+MESH = pl.DeviceIdType.MESH
 
 HEAD_DIM = 128
 
@@ -234,6 +241,475 @@
     return (velocity, colours.transpose(2, 0, 1))
 
 
+def contract_last(left, right):
+    return lax.dot_general(
+        left, right, (((1,), (1,)), ((), ())), preferred_element_type=jnp.float32
+    )
+
+
+def fused(
+    count,
+    kb_s, ms_s, guide_s,
+    q_hbm, k_hbm, v_hbm, kt_hbm, mt_hbm, ow_hbm, lat_hbm, ci_hbm, gain_hbm, co_hbm,
+    vel_out, rgb_out,
+    qs, ks, vs, rq, rk, rv, kt, mt, ow, lat, ci, gain, co,
+    act, kbias, wts, psend, precv, ext, late, wbig, vt, weave,
+    local_sem, send_sem, recv_sem, send2, recv2, lat_send, lat_recv, x_send, x_recv,
+):
+    me = lax.axis_index("tok")
+    core = lax.axis_index("branch")
+    other = 1 - core
+    rows = q_hbm.shape[0]
+    half = rows // 2
+    cols = rq.shape[1]
+    heads = cols // HEAD_DIM
+    tokens = rows * count
+    patch = lat_hbm.shape[1]
+    dec = gain.shape[0]
+    lat_ch = ci.shape[0] // 9
+    below = lax.rem(me + count - 1, count)
+    above = lax.rem(me + 1, count)
+    has_low = me > 0
+    has_high = me < count - 1
+
+    def span(index):
+        return pl.ds(pl.multiple_of((2 * index + core) * cols, cols), cols)
+
+    def own_rows(index):
+        return pl.ds(pl.multiple_of(index * rows, rows), rows)
+
+    ext[...] = jnp.zeros_like(ext)
+    late[0] = jnp.zeros(late.shape[1:], late.dtype)
+    late[2] = jnp.zeros(late.shape[1:], late.dtype)
+    barrier = pltpu.get_barrier_semaphore()
+    for step in range(1, count):
+        pl.semaphore_signal(
+            barrier, inc=1, device_id={"tok": lax.rem(me + step, count)}, device_id_type=MESH
+        )
+    pl.semaphore_signal(barrier, inc=1, device_id={"branch": other}, device_id_type=MESH)
+    for peer in (below, above):
+        pl.semaphore_signal(
+            barrier, inc=1, device_id={"tok": peer, "branch": other}, device_id_type=MESH
+        )
+
+    loads = [
+        pltpu.make_async_copy(q_hbm, qs, local_sem.at[0]),
+        pltpu.make_async_copy(k_hbm, ks, local_sem.at[1]),
+        pltpu.make_async_copy(v_hbm, vs, local_sem.at[2]),
+        pltpu.make_async_copy(lat_hbm, lat, local_sem.at[3]),
+        pltpu.make_async_copy(q_hbm.at[:, span(me)], rq.at[own_rows(me), :], local_sem.at[4]),
+        pltpu.make_async_copy(k_hbm.at[:, span(me)], rk.at[own_rows(me), :], local_sem.at[5]),
+        pltpu.make_async_copy(v_hbm.at[:, span(me)], rv.at[own_rows(me), :], local_sem.at[6]),
+        pltpu.make_async_copy(kt_hbm.at[:, :, span(me)], kt, local_sem.at[7]),
+        pltpu.make_async_copy(mt_hbm.at[:, :, span(me)], mt, local_sem.at[8]),
+        pltpu.make_async_copy(ow_hbm.at[:, span(me)], ow, local_sem.at[9]),
+        pltpu.make_async_copy(ci_hbm, ci, local_sem.at[10]),
+        pltpu.make_async_copy(gain_hbm, gain, local_sem.at[11]),
+        pltpu.make_async_copy(co_hbm, co, local_sem.at[12]),
+    ]
+    for load in loads:
+        load.start()
+    for load in loads[:4]:
+        load.wait()
+    late[1] = jnp.concatenate([lat[:half, :], lat[half:, :]], axis=1)
+
+    pl.semaphore_wait(barrier, count + 2)
+
+    sends = []
+    for which, (source, target) in enumerate(((qs, rq), (ks, rk), (vs, rv))):
+        for step in range(1, count):
+            peer = lax.rem(me + step, count)
+            copy = pltpu.make_async_remote_copy(
+                src_ref=source.at[:, span(peer)],
+                dst_ref=target.at[own_rows(me), :],
+                send_sem=send_sem.at[which, step],
+                recv_sem=recv_sem.at[which, me],
+                device_id={"tok": peer},
+                device_id_type=MESH,
+            )
+            copy.start()
+            sends.append(copy)
+
+    def latent_copy(peer, slot):
+        return pltpu.make_async_remote_copy(
+            src_ref=late.at[1],
+            dst_ref=late.at[slot],
+            send_sem=lat_send.at[slot],
+            recv_sem=lat_recv.at[slot],
+            device_id={"tok": peer},
+            device_id_type=MESH,
+        )
+
+    @pl.when(has_low)
+    def _():
+        latent_copy(below, 2).start()
+
+    @pl.when(has_high)
+    def _():
+        latent_copy(above, 0).start()
+
+    def arrived(which, target):
+        for step in range(1, count):
+            peer = lax.rem(me + step, count)
+            pltpu.make_async_remote_copy(
+                src_ref=target.at[own_rows(peer), :],
+                dst_ref=target.at[own_rows(peer), :],
+                send_sem=send_sem.at[which, step],
+                recv_sem=recv_sem.at[which, peer],
+                device_id={"tok": peer},
+                device_id_type=MESH,
+            ).wait_recv()
+
+    for load in loads[4:]:
+        load.wait()
+    for frame in range(count):
+        key_rows = kt[kb_s[frame]].astype(jnp.float32)
+        mouse_rows = mt[ms_s[frame]].astype(jnp.float32)
+        for which, term in enumerate((key_rows + mouse_rows, mouse_rows, key_rows)):
+            for part in range(2):
+                act[part, which, frame : frame + 1, :] = term[part : part + 1, :]
+    for which in range(3):
+        spread = jnp.broadcast_to(act[0, which][:, None, :], (count, rows, cols))
+        kbias[which] = spread.reshape(tokens, cols).astype(jnp.bfloat16)
+    wbig[...] = jnp.zeros_like(wbig)
+    for place in range(2):
+        for shift in range(2):
+            out_at = (place * 2 + shift) * dec
+            for first in range(3):
+                for second in range(3):
+                    line, column = place + first, shift + second
+                    second_half = column in (0, 3)
+                    part = {0: 1, 1: 0, 2: 1, 3: 0}[column]
+                    at = second_half * 2 * patch + line * 2 * lat_ch + part * lat_ch
+                    from_at = (first * 3 + second) * lat_ch
+                    wbig[at : at + lat_ch, out_at : out_at + dec] = ci[
+                        from_at : from_at + lat_ch, :
+                    ]
+    colour_count = co.shape[1]
+    spare = jnp.zeros((8 - colour_count, dec), jnp.float32)
+    padded = [part for at in range(9) for part in (co[at].astype(jnp.float32), spare)]
+    vt[...] = jnp.concatenate(padded, axis=0).astype(jnp.bfloat16)
+    from_lane = lax.broadcasted_iota(jnp.int32, weave.shape, 0)
+    to_lane = lax.broadcasted_iota(jnp.int32, weave.shape, 1)
+    from_at = lax.rem(from_lane, 4 * rows)
+    woven = 2 * from_at + from_lane // (4 * rows)
+    weave[...] = jnp.where((woven == to_lane) & (from_at < 2 * rows), 1.0, 0.0).astype(
+        jnp.bfloat16
+    )
+
+    arrived(0, rq)
+    arrived(1, rk)
+    factor = HEAD_DIM ** (-0.5) * math.log2(math.e)
+    totals = []
+    for head in range(heads):
+        lanes = slice(head * HEAD_DIM, (head + 1) * HEAD_DIM)
+        query = rq[:, lanes]
+        key = rk[:, lanes]
+        both = jnp.concatenate([query, query], axis=1)
+        for which in range(4):
+            if which < 3:
+                scores = contract_last(
+                    both, jnp.concatenate([key, kbias[which, :, lanes]], axis=1)
+                )
+            else:
+                scores = contract_last(query, key)
+            top = jnp.max(scores, axis=1, keepdims=True)
+            raised = jnp.exp2((scores - top) * factor)
+            totals.append(jnp.sum(raised, axis=1, keepdims=True))
+            wts[head * 4 + which] = raised.astype(jnp.bfloat16)
+    arrived(2, rv)
+    combined = []
+    for head in range(heads):
+        lanes = slice(head * HEAD_DIM, (head + 1) * HEAD_DIM)
+        plain = rv[:, lanes].astype(jnp.float32).reshape(count, rows, HEAD_DIM)
+        mixed = None
+        for which in range(4):
+            if which < 3:
+                value = plain + act[1, which, :, lanes][:, None, :]
+                value = value.reshape(tokens, HEAD_DIM).astype(jnp.bfloat16)
+            else:
+                value = rv[:, lanes]
+            summed = jnp.dot(wts[head * 4 + which], value, preferred_element_type=jnp.float32)
+            attended = (summed / totals[head * 4 + which]).astype(jnp.bfloat16)
+            term = guide_s[which] * attended.astype(jnp.float32)
+            mixed = term if mixed is None else mixed + term
+        combined.append(mixed.astype(jnp.bfloat16))
+    joined = jnp.concatenate(combined, axis=1).reshape(count, 2, half, cols)
+    blank = jnp.zeros(ow.shape, ow.dtype)
+    left_weight = jnp.concatenate([ow[...], blank], axis=0)
+    right_weight = jnp.concatenate([blank, ow[...]], axis=0)
+    part_sums = contract_last(
+        joined[:, 0].reshape(count * half, cols), left_weight
+    ) + contract_last(joined[:, 1].reshape(count * half, cols), right_weight)
+    psend[...] = part_sums.reshape(count, half, 2 * patch).astype(psend.dtype)
+
+    for step in range(1, count):
+        peer = lax.rem(me + step, count)
+        copy = pltpu.make_async_remote_copy(
+            src_ref=psend.at[peer],
+            dst_ref=precv.at[me],
+            send_sem=send2.at[step],
+            recv_sem=recv2.at[me],
+            device_id={"tok": peer},
+            device_id_type=MESH,
+        )
+        copy.start()
+        sends.append(copy)
+    precv[me] = psend[me]
+    for step in range(1, count):
+        peer = lax.rem(me + step, count)
+        pltpu.make_async_remote_copy(
+            src_ref=psend.at[peer],
+            dst_ref=precv.at[peer],
+            send_sem=send2.at[step],
+            recv_sem=recv2.at[peer],
+            device_id={"tok": peer},
+            device_id_type=MESH,
+        ).wait_recv()
+    ext[1, core] = jnp.sum(precv[...].astype(jnp.float32), axis=0)
+
+    def exchange(at, slot, where):
+        return pltpu.make_async_remote_copy(
+            src_ref=ext.at[1, core],
+            dst_ref=ext.at[slot, core],
+            send_sem=x_send.at[at],
+            recv_sem=x_recv.at[slot, core],
+            device_id=where,
+            device_id_type=MESH,
+        )
+
+    def expect(slot, branch):
+        pltpu.make_async_remote_copy(
+            src_ref=ext.at[1, core],
+            dst_ref=ext.at[slot, branch],
+            send_sem=x_send.at[0],
+            recv_sem=x_recv.at[slot, branch],
+            device_id={"branch": other},
+            device_id_type=MESH,
+        ).wait_recv()
+
+    low_copies = [
+        exchange(1, 2, {"tok": below, "branch": core}),
+        exchange(2, 2, {"tok": below, "branch": other}),
+    ]
+    high_copies = [
+        exchange(3, 0, {"tok": above, "branch": core}),
+        exchange(4, 0, {"tok": above, "branch": other}),
+    ]
+    across = exchange(0, 1, {"branch": other})
+
+    @pl.when(has_low)
+    def _():
+        for copy in low_copies:
+            copy.start()
+
+    @pl.when(has_high)
+    def _():
+        for copy in high_copies:
+            copy.start()
+
+    across.start()
+    expect(1, other)
+
+    @pl.when(has_low)
+    def _():
+        latent_copy(below, 0).wait_recv()
+        expect(0, 0)
+        expect(0, 1)
+
+    @pl.when(has_high)
+    def _():
+        latent_copy(above, 2).wait_recv()
+        expect(2, 0)
+        expect(2, 1)
+
+    velocity = ext[:, 0] + ext[:, 1]
+    vel_out[:half, :] = velocity[1][:, :patch]
+    vel_out[half:, :] = velocity[1][:, patch:]
+    stepped = late[...] - step_size * velocity
+    stepped = stepped.astype(jnp.bfloat16).astype(jnp.float32)
+    lane = lax.broadcasted_iota(jnp.int32, (half, 2 * patch), 1)
+    row = lax.broadcasted_iota(jnp.int32, (rows, 2 * patch), 0)
+    wide = lax.broadcasted_iota(jnp.int32, (rows, 2 * patch), 1)
+    blocks = []
+    for low in range(2):
+        one, two = stepped[low], stepped[low + 1]
+        pair = jnp.concatenate(
+            [
+                jnp.where(lane < patch, one, pltpu.roll(two, patch, 1)),
+                jnp.where(lane < patch, pltpu.roll(one, patch, 1), two),
+            ],
+            axis=0,
+        )
+        before = jnp.where(row == 0, 0.0, pltpu.roll(pair, 1, 0))
+        after = jnp.where(row == rows - 1, 0.0, pltpu.roll(pair, rows - 1, 0))
+        sides = jnp.where(lax.rem(wide, 2 * lat_ch) < lat_ch, after, before)
+        blocks.append(jnp.concatenate([pair, sides], axis=1))
+    windows = jnp.concatenate(blocks, axis=0).astype(jnp.bfloat16)
+    gained = gain[...].reshape(1, dec)
+    taps = []
+    for shift in range(2):
+        lines = []
+        for place in range(2):
+            out_at = (place * 2 + shift) * dec
+            features = jnp.dot(
+                windows, wbig[:, out_at : out_at + dec], preferred_element_type=jnp.float32
+            )
+            square = jnp.mean(features * features, axis=1, keepdims=True)
+            scaled = features * lax.rsqrt(square + norm_eps) * gained
+            lines.append(scaled / (1.0 + jnp.exp(-scaled)))
+        ordered = jnp.concatenate(
+            [
+                jnp.where(has_low, lines[0][:rows], 0.0),
+                lines[1][:rows],
+                lines[0][rows:],
+                jnp.where(has_high, lines[1][rows:], 0.0),
+            ],
+            axis=0,
+        ).astype(jnp.bfloat16)
+        taps.append(contract_last(vt[...], ordered))
+    inner = lax.rem(lax.broadcasted_iota(jnp.int32, (8, 4 * rows), 1), rows)
+
+    def tap(shift, first, second):
+        at = (first * 3 + second) * 8
+        return taps[shift][at : at + 8, :]
+
+    halves = []
+    for shift in range(2):
+        out = None
+        for first in range(3):
+            if shift == 0:
+                edge = jnp.where(inner == 0, 0.0, pltpu.roll(tap(1, first, 0), 1, 1))
+                line = tap(0, first, 1) + tap(1, first, 2) + edge
+            else:
+                edge = jnp.where(
+                    inner == rows - 1, 0.0, pltpu.roll(tap(0, first, 2), 4 * rows - 1, 1)
+                )
+                line = tap(0, first, 0) + tap(1, first, 1) + edge
+            if first > 0:
+                line = pltpu.roll(line, (4 - first) * rows, 1)
+            out = line if out is None else out + line
+        halves.append(out)
+    rest = jnp.concatenate(halves, axis=1)
+    parts = []
+    for _ in range(3):
+        parts.append(rest.astype(jnp.bfloat16).astype(jnp.float32))
+        rest = rest - parts[-1]
+    moved = jnp.dot(
+        jnp.concatenate(parts, axis=0).astype(jnp.bfloat16),
+        weave[...],
+        preferred_element_type=jnp.float32,
+    )
+    colours = moved[:8] + moved[8:16] + moved[16:]
+    for line in range(2):
+        rgb_out[:, line, :] = colours[:colour_count, line * 2 * rows : (line + 1) * 2 * rows]
+
+    for copy in sends:
+        copy.wait_send()
+    across.wait_send()
+
+    @pl.when(has_low)
+    def _():
+        latent_copy(below, 2).wait_send()
+        for copy in low_copies:
+            copy.wait_send()
+
+    @pl.when(has_high)
+    def _():
+        latent_copy(above, 0).wait_send()
+        for copy in high_copies:
+            copy.wait_send()
+
+
+def fused_shards(
+    queries,
+    keys,
+    values,
+    keyboard,
+    mouse,
+    key_table,
+    mouse_table,
+    guidance,
+    out_weight,
+    latent,
+    conv_in,
+    gain,
+    conv_out,
+):
+    count = lax.axis_size("tok")
+    rows, width = queries.shape
+    cols = width // (2 * count)
+    tokens = rows * count
+    patch = latent.shape[1]
+    lat_ch, dec = conv_in.shape[2:]
+    colours = conv_out.shape[3]
+    half = rows // 2
+    bf16, f32 = jnp.bfloat16, jnp.float32
+    smem = pl.BlockSpec(memory_space=pltpu.SMEM)
+    anywhere = pl.BlockSpec(memory_space=pl.ANY)
+    vmem = pl.BlockSpec(memory_space=pltpu.VMEM)
+    dma = pltpu.SemaphoreType.DMA
+    velocity, rgb = pl.pallas_call(
+        functools.partial(fused, count),
+        out_shape=(
+            jax.ShapeDtypeStruct((rows, patch), f32),
+            jax.ShapeDtypeStruct((colours, 2, 2 * rows), f32),
+        ),
+        in_specs=[smem] * 3 + [anywhere] * 10,
+        out_specs=(vmem, vmem),
+        scratch_shapes=[
+            pltpu.VMEM((rows, width), bf16),
+            pltpu.VMEM((rows, width), bf16),
+            pltpu.VMEM((rows, width), bf16),
+            pltpu.VMEM((tokens, cols), bf16),
+            pltpu.VMEM((tokens, cols), bf16),
+            pltpu.VMEM((tokens, cols), bf16),
+            pltpu.VMEM((key_table.shape[0], 2, cols), bf16),
+            pltpu.VMEM((mouse_table.shape[0], 2, cols), bf16),
+            pltpu.VMEM((patch, cols), bf16),
+            pltpu.VMEM((rows, patch), f32),
+            pltpu.VMEM((9 * lat_ch, dec), bf16),
+            pltpu.VMEM((dec,), f32),
+            pltpu.VMEM((9, colours, dec), bf16),
+            pltpu.VMEM((2, 3, count, cols), f32),
+            pltpu.VMEM((3, tokens, cols), bf16),
+            pltpu.VMEM((4 * cols // HEAD_DIM, tokens, tokens), bf16),
+            pltpu.VMEM((count, half, 2 * patch), bf16),
+            pltpu.VMEM((count, half, 2 * patch), bf16),
+            pltpu.VMEM((3, 2, half, 2 * patch), f32),
+            pltpu.VMEM((3, half, 2 * patch), f32),
+            pltpu.VMEM((4 * patch, 4 * dec), bf16),
+            pltpu.VMEM((72, dec), bf16),
+            pltpu.VMEM((8 * rows, 4 * rows), bf16),
+            dma((13,)),
+            dma((3, count)),
+            dma((3, count)),
+            dma((count,)),
+            dma((count,)),
+            dma((3,)),
+            dma((3,)),
+            dma((5,)),
+            dma((3, 2)),
+        ],
+        compiler_params=pltpu.CompilerParams(collective_id=0, has_side_effects=True),
+    )(
+        keyboard,
+        mouse,
+        guidance,
+        queries,
+        keys,
+        values,
+        key_table,
+        mouse_table,
+        out_weight.T,
+        latent,
+        conv_in.reshape(9 * lat_ch, dec),
+        gain,
+        conv_out.transpose(0, 1, 3, 2).reshape(9, colours, dec),
+    )
+    return velocity, rgb
+
+
 def solution(mesh):
     placed = (
         P(("groups", "tok"), None),
@@ -250,8 +726,15 @@
         P(),
         P(),
     )
+
+    def step(queries, keys, values, keyboard, *rest):
+        count = lax.axis_size("tok")
+        single = count == 8 and keyboard.shape[0] == count
+        body = fused_shards if single else shards
+        return body(queries, keys, values, keyboard, *rest)
+
     return jax.shard_map(
-        shards,
+        step,
         mesh=mesh,
         in_specs=placed,
         out_specs=(P(("groups", "tok"), None), P(None, ("groups", "tok"), None)),

time: 85.4 us -> 29.4 us (0.34)
  the two profiles are of different devices: /device:TPU:8 before, /device:TPU:0 now
where the time goes in v1:
time: 29.4 us; the launch traced here: 29.2 us
  Pallas kernels  26.6 us (90%)
  local copies, waits for them, and re-layouts  1.91 us (6%)
  between operations  0.65 us (2%)
    pallas_call x1, Pallas kernels, fused_shards(): pl.pallas_call(functools.partial(fused, count), out_shape=(jax.ShapeDtype...  26.6 us
    unnamed x4, local copies, waits for them, and re-layouts  1.91 us

profile of v1, /device:TPU:0, one launch (start us, length us, event | category | flops | bytes accessed | tf_op | source)
XLA Modules:
  0.0 29.2 jit_solution(3692894278551368631)
XLA Ops:
  0.6 26.6 %shard_map.140 = (f32[32,64]{1,0:T(8,128)}, f32[3,2,64]{2,1,0:T(2,128)}) custom-call(s32[8]{0:T(128)} %kb_s.1, s32[8]{0:T(128)} %ms_s.1, f32[4]{0:T(128)} %guide_s.1, bf16[32,4096]{1,0:T(8,128)(2,1)} %q_hbm.1, bf16[32,4096]{1,0:T(8,128)(2,1)} %k_hbm.1, bf16[32,4096]{1,0:T(8,128)(2,1)} %v_hbm.1, bf16[16,2,4096]{2,1,0:T(2,128)(2,1)} %kt_hbm.1, ...), custom_call_target="tpu_custom_call" | custom-call | tf_op jit(solution)/shard_map/pallas_call | solution.py:652
  27.2 0.0 copy-start
  27.2 1.3 %copy.17 = f32[32,64]{1,0:T(8,128)} copy(f32[32,64]{1,0:T(8,128)} %get-tuple-element.4) | data formatting | bytes 16384
  28.6 0.0 copy-done
  28.6 0.6 %copy.18 = f32[3,2,64]{2,1,0:T(2,128)} copy(f32[3,2,64]{2,1,0:T(2,128)S(1)} %copy-done) | data formatting | bytes 3072
Async XLA Ops:
  27.2 1.3 %copy-start = (f32[3,2,64]{2,1,0:T(2,128)S(1)}, f32[3,2,64]{2,1,0:T(2,128)}, u32[]{:S(2)}) copy-start(f32[3,2,64]{2,1,0:T(2,128)} %get-tuple-element.5) | copy-start | bytes 4612

commit v2 on v1

--- a/solution.py
+++ b/solution.py
@@ -249,12 +249,12 @@
 
 def fused(
     count,
-    kb_s, ms_s, guide_s,
+    kb_hbm, ms_hbm, guide_hbm,
     q_hbm, k_hbm, v_hbm, kt_hbm, mt_hbm, ow_hbm, lat_hbm, ci_hbm, gain_hbm, co_hbm,
     vel_out, rgb_out,
-    qs, ks, vs, rq, rk, rv, kt, mt, ow, lat, ci, gain, co,
+    kb_s, ms_s, guide_s, qs, ks, vs, rq, rk, rv, kt, mt, ow, lat, ci, gain, co,
     act, kbias, wts, psend, precv, ext, late, wbig, vt, weave,
-    local_sem, send_sem, recv_sem, send2, recv2, lat_send, lat_recv, x_send, x_recv,
+    local_sem, send_sem, recv_sem, send2, recv2, lat_send, lat_recv, x_send, x_recv, relay,
 ):
     me = lax.axis_index("tok")
     core = lax.axis_index("branch")
@@ -272,6 +272,21 @@
     has_low = me > 0
     has_high = me < count - 1
 
+    plane, side = lax.div(me, 2), lax.rem(me, 2)
+    beside = plane + 1 - 2 * lax.rem(plane, 2)
+    opposite = plane + 2 - 4 * lax.div(plane, 2)
+    mirror = 3 - plane
+    middle = (plane == 1) | (plane == 2)
+    near = [
+        2 * opposite + side,
+        2 * beside + 1 - side,
+        2 * beside + side,
+        2 * plane + 1 - side,
+    ]
+    facing = [2 * mirror + side, 2 * mirror + 1 - side]
+    distant = 2 * opposite + 1 - side
+    peers = facing + [distant] + near
+
     def span(index):
         return pl.ds(pl.multiple_of((2 * index + core) * cols, cols), cols)
 
@@ -282,15 +297,22 @@
     late[0] = jnp.zeros(late.shape[1:], late.dtype)
     late[2] = jnp.zeros(late.shape[1:], late.dtype)
     barrier = pltpu.get_barrier_semaphore()
-    for step in range(1, count):
-        pl.semaphore_signal(
-            barrier, inc=1, device_id={"tok": lax.rem(me + step, count)}, device_id_type=MESH
-        )
+    for peer in near:
+        pl.semaphore_signal(barrier, inc=1, device_id={"tok": peer}, device_id_type=MESH)
     pl.semaphore_signal(barrier, inc=1, device_id={"branch": other}, device_id_type=MESH)
-    for peer in (below, above):
-        pl.semaphore_signal(
-            barrier, inc=1, device_id={"tok": peer, "branch": other}, device_id_type=MESH
-        )
+
+    @pl.when(middle)
+    def _():
+        for peer in facing:
+            pl.semaphore_signal(barrier, inc=1, device_id={"tok": peer}, device_id_type=MESH)
+
+    for exists, peer in ((has_low, below), (has_high, above)):
+
+        @pl.when(exists)
+        def _(peer=peer):
+            pl.semaphore_signal(
+                barrier, inc=1, device_id={"tok": peer, "branch": other}, device_id_type=MESH
+            )
 
     loads = [
         pltpu.make_async_copy(q_hbm, qs, local_sem.at[0]),
@@ -306,6 +328,9 @@
         pltpu.make_async_copy(ci_hbm, ci, local_sem.at[10]),
         pltpu.make_async_copy(gain_hbm, gain, local_sem.at[11]),
         pltpu.make_async_copy(co_hbm, co, local_sem.at[12]),
+        pltpu.make_async_copy(kb_hbm, kb_s, local_sem.at[13]),
+        pltpu.make_async_copy(ms_hbm, ms_s, local_sem.at[14]),
+        pltpu.make_async_copy(guide_hbm, guide_s, local_sem.at[15]),
     ]
     for load in loads:
         load.start()
@@ -313,22 +338,34 @@
         load.wait()
     late[1] = jnp.concatenate([lat[:half, :], lat[half:, :]], axis=1)
 
-    pl.semaphore_wait(barrier, count + 2)
-
-    sends = []
-    for which, (source, target) in enumerate(((qs, rq), (ks, rk), (vs, rv))):
-        for step in range(1, count):
-            peer = lax.rem(me + step, count)
-            copy = pltpu.make_async_remote_copy(
-                src_ref=source.at[:, span(peer)],
-                dst_ref=target.at[own_rows(me), :],
-                send_sem=send_sem.at[which, step],
-                recv_sem=recv_sem.at[which, me],
-                device_id={"tok": peer},
-                device_id_type=MESH,
-            )
-            copy.start()
-            sends.append(copy)
+    def flag(condition):
+        return jnp.where(condition, 1, 0)
+
+    pl.semaphore_wait(barrier, 5 + 2 * flag(middle) + flag(has_low) + flag(has_high))
+    pl.semaphore_signal(relay, inc=1, device_id={"tok": near[0]}, device_id_type=MESH)
+
+    moves = ((qs, rq), (ks, rk), (vs, rv))
+
+    def block_copy(which, at):
+        source, target = moves[which]
+        return pltpu.make_async_remote_copy(
+            src_ref=source.at[:, span(peers[at])],
+            dst_ref=target.at[own_rows(me), :],
+            send_sem=send_sem.at[which, at],
+            recv_sem=recv_sem.at[which, me],
+            device_id={"tok": peers[at]},
+            device_id_type=MESH,
+        )
+
+    @pl.when(middle)
+    def _():
+        for which in range(2):
+            for at in range(2):
+                block_copy(which, at).start()
+
+    for which in range(2):
+        for at in range(3, count - 1):
+            block_copy(which, at).start()
 
     def latent_copy(peer, slot):
         return pltpu.make_async_remote_copy(
@@ -348,9 +385,22 @@
     def _():
         latent_copy(above, 0).start()
 
+    pl.semaphore_wait(relay, 1)
+
+    @pl.when(jnp.logical_not(middle))
+    def _():
+        for which in range(2):
+            for at in range(2):
+                block_copy(which, at).start()
+
+    for which in range(2):
+        block_copy(which, 2).start()
+    for at in range(count - 1):
+        block_copy(2, at).start()
+    sends = [block_copy(which, at) for which in range(3) for at in range(count - 1)]
+
     def arrived(which, target):
-        for step in range(1, count):
-            peer = lax.rem(me + step, count)
+        for step, peer in enumerate(peers):
             pltpu.make_async_remote_copy(
                 src_ref=target.at[own_rows(peer), :],
                 dst_ref=target.at[own_rows(peer), :],
@@ -443,8 +493,7 @@
     ) + contract_last(joined[:, 1].reshape(count * half, cols), right_weight)
     psend[...] = part_sums.reshape(count, half, 2 * patch).astype(psend.dtype)
 
-    for step in range(1, count):
-        peer = lax.rem(me + step, count)
+    for step, peer in enumerate(peers):
         copy = pltpu.make_async_remote_copy(
             src_ref=psend.at[peer],
             dst_ref=precv.at[me],
@@ -456,8 +505,7 @@
         copy.start()
         sends.append(copy)
     precv[me] = psend[me]
-    for step in range(1, count):
-        peer = lax.rem(me + step, count)
+    for step, peer in enumerate(peers):
         pltpu.make_async_remote_copy(
             src_ref=psend.at[peer],
             dst_ref=precv.at[peer],
@@ -645,19 +693,25 @@
     colours = conv_out.shape[3]
     half = rows // 2
     bf16, f32 = jnp.bfloat16, jnp.float32
-    smem = pl.BlockSpec(memory_space=pltpu.SMEM)
-    anywhere = pl.BlockSpec(memory_space=pl.ANY)
+    hbm = pl.BlockSpec(memory_space=pltpu.HBM)
     vmem = pl.BlockSpec(memory_space=pltpu.VMEM)
     dma = pltpu.SemaphoreType.DMA
+
+    def pin(array):
+        return pltpu.with_memory_space_constraint(array, pltpu.HBM)
+
     velocity, rgb = pl.pallas_call(
         functools.partial(fused, count),
         out_shape=(
             jax.ShapeDtypeStruct((rows, patch), f32),
             jax.ShapeDtypeStruct((colours, 2, 2 * rows), f32),
         ),
-        in_specs=[smem] * 3 + [anywhere] * 10,
+        in_specs=[hbm] * 13,
         out_specs=(vmem, vmem),
         scratch_shapes=[
+            pltpu.SMEM(keyboard.shape, jnp.int32),
+            pltpu.SMEM(mouse.shape, jnp.int32),
+            pltpu.SMEM(guidance.shape, f32),
             pltpu.VMEM((rows, width), bf16),
             pltpu.VMEM((rows, width), bf16),
             pltpu.VMEM((rows, width), bf16),
@@ -681,7 +735,7 @@
             pltpu.VMEM((4 * patch, 4 * dec), bf16),
             pltpu.VMEM((72, dec), bf16),
             pltpu.VMEM((8 * rows, 4 * rows), bf16),
-            dma((13,)),
+            dma((16,)),
             dma((3, count)),
             dma((3, count)),
             dma((count,)),
@@ -690,22 +744,23 @@
             dma((3,)),
             dma((5,)),
             dma((3, 2)),
+            pltpu.SemaphoreType.REGULAR,
         ],
-        compiler_params=pltpu.CompilerParams(collective_id=0, has_side_effects=True),
+        compiler_params=pltpu.CompilerParams(collective_id=0, has_side_effects=True, vmem_limit_bytes=16 * 2**20),
     )(
-        keyboard,
-        mouse,
-        guidance,
-        queries,
-        keys,
-        values,
-        key_table,
-        mouse_table,
-        out_weight.T,
-        latent,
-        conv_in.reshape(9 * lat_ch, dec),
-        gain,
-        conv_out.transpose(0, 1, 3, 2).reshape(9, colours, dec),
+        pin(keyboard),
+        pin(mouse),
+        pin(guidance),
+        pin(queries),
+        pin(keys),
+        pin(values),
+        pin(key_table),
+        pin(mouse_table),
+        pin(out_weight.T),
+        pin(latent),
+        pin(conv_in.reshape(9 * lat_ch, dec)),
+        pin(gain),
+        pin(conv_out.transpose(0, 1, 3, 2).reshape(9, colours, dec)),
     )
     return velocity, rgb
 

time: 29.4 us -> 27.5 us (0.935)
  Pallas kernels: 26.6 us -> 25.5 us
  local copies, waits for them, and re-layouts: 1.91 us -> 1.19 us
    pallas_call x1, Pallas kernels: 26.6 us -> 25.5 us  [fused_shards(): pl.pallas_call(functools.partial(fused, count), out_shape=(jax.ShapeDtype...]
    unnamed x4 -> x2, local copies, waits for them, and re-layouts: 1.91 us -> 1.19 us
where the time goes in v2:
time: 27.5 us; the launch traced here: 27.4 us
  Pallas kernels  25.5 us (93%)
  local copies, waits for them, and re-layouts  1.19 us (4%)
  between operations  0.64 us (2%)
    pallas_call x1, Pallas kernels, fused_shards(): pl.pallas_call(functools.partial(fused, count), out_shape=(jax.ShapeDtype...  25.5 us
    unnamed x2, local copies, waits for them, and re-layouts  1.19 us

profile of v2, /device:TPU:0, one launch (start us, length us, event | category | flops | bytes accessed | tf_op | source)
XLA Modules:
  0.0 27.4 jit_solution(17782732908302922344)
XLA Ops:
  0.6 25.5 %shard_map.140 = (f32[32,64]{1,0:T(8,128)S(1)}, f32[3,2,64]{2,1,0:T(2,128)S(1)}) custom-call(s32[8]{0:T(128)} %kb_hbm.1, s32[8]{0:T(128)} %ms_hbm.1, f32[4]{0:T(128)} %guide_hbm.1, bf16[32,4096]{1,0:T(8,128)(2,1)} %q_hbm.1, bf16[32,4096]{1,0:T(8,128)(2,1)} %k_hbm.1, bf16[32,4096]{1,0:T(8,128)(2,1)} %v_hbm.1, bf16[16,2,4096]{2,1,0:T(2,128)(2,1)} %kt_hbm.1, ...), custom_call_target="tpu_custom_call" | custom-call | tf_op jit(solution)/shard_map/pallas_call | solution.py:703
  26.2 0.6 %copy.17 = f32[32,64]{1,0:T(8,128)} copy(f32[32,64]{1,0:T(8,128)S(1)} %get-tuple-element.4) | data formatting | bytes 16384
  26.8 0.6 %copy.18 = f32[3,2,64]{2,1,0:T(2,128)} copy(f32[3,2,64]{2,1,0:T(2,128)S(1)} %get-tuple-element.5) | data formatting | bytes 3072

commit v3 on v2

--- a/solution.py
+++ b/solution.py
@@ -252,7 +252,7 @@
     kb_hbm, ms_hbm, guide_hbm,
     q_hbm, k_hbm, v_hbm, kt_hbm, mt_hbm, ow_hbm, lat_hbm, ci_hbm, gain_hbm, co_hbm,
     vel_out, rgb_out,
-    kb_s, ms_s, guide_s, qs, ks, vs, rq, rk, rv, kt, mt, ow, lat, ci, gain, co,
+    kb_s, ms_s, guide_s, qs, ks, vs, rq, rk, rv, kt, mt, ow, vw, lat, ci, gain, co,
     act, kbias, wts, psend, precv, ext, late, wbig, vt, weave,
     local_sem, send_sem, recv_sem, send2, recv2, lat_send, lat_recv, x_send, x_recv, relay,
 ):
@@ -321,10 +321,9 @@
         pltpu.make_async_copy(lat_hbm, lat, local_sem.at[3]),
         pltpu.make_async_copy(q_hbm.at[:, span(me)], rq.at[own_rows(me), :], local_sem.at[4]),
         pltpu.make_async_copy(k_hbm.at[:, span(me)], rk.at[own_rows(me), :], local_sem.at[5]),
-        pltpu.make_async_copy(v_hbm.at[:, span(me)], rv.at[own_rows(me), :], local_sem.at[6]),
         pltpu.make_async_copy(kt_hbm.at[:, :, span(me)], kt, local_sem.at[7]),
         pltpu.make_async_copy(mt_hbm.at[:, :, span(me)], mt, local_sem.at[8]),
-        pltpu.make_async_copy(ow_hbm.at[:, span(me)], ow, local_sem.at[9]),
+        pltpu.make_async_copy(ow_hbm, ow, local_sem.at[9]),
         pltpu.make_async_copy(ci_hbm, ci, local_sem.at[10]),
         pltpu.make_async_copy(gain_hbm, gain, local_sem.at[11]),
         pltpu.make_async_copy(co_hbm, co, local_sem.at[12]),
@@ -349,7 +348,7 @@
     def block_copy(which, at):
         source, target = moves[which]
         return pltpu.make_async_remote_copy(
-            src_ref=source.at[:, span(peers[at])],
+            src_ref=vw.at[peers[at]] if which == 2 else source.at[:, span(peers[at])],
             dst_ref=target.at[own_rows(me), :],
             send_sem=send_sem.at[which, at],
             recv_sem=recv_sem.at[which, me],
@@ -395,6 +394,19 @@
 
     for which in range(2):
         block_copy(which, 2).start()
+    for load in loads[4:]:
+        load.wait()
+    for index in range(count):
+        block, weight = vs[:, span(index)], ow[:, span(index)]
+        ahead = [
+            contract_last(
+                block[:, at * HEAD_DIM : (at + 1) * HEAD_DIM],
+                weight[:, at * HEAD_DIM : (at + 1) * HEAD_DIM],
+            )
+            for at in range(heads)
+        ]
+        vw[index] = jnp.concatenate(ahead, axis=1).astype(vw.dtype)
+    rv[own_rows(me), :] = vw[me]
     for at in range(count - 1):
         block_copy(2, at).start()
     sends = [block_copy(which, at) for which in range(3) for at in range(count - 1)]
@@ -410,8 +422,6 @@
                 device_id_type=MESH,
             ).wait_recv()
 
-    for load in loads[4:]:
-        load.wait()
     for frame in range(count):
         key_rows = kt[kb_s[frame]].astype(jnp.float32)
         mouse_rows = mt[ms_s[frame]].astype(jnp.float32)
@@ -468,30 +478,25 @@
             totals.append(jnp.sum(raised, axis=1, keepdims=True))
             wts[head * 4 + which] = raised.astype(jnp.bfloat16)
     arrived(2, rv)
-    combined = []
+    own_weight = ow[:, span(me)]
+    part_sums = None
     for head in range(heads):
         lanes = slice(head * HEAD_DIM, (head + 1) * HEAD_DIM)
-        plain = rv[:, lanes].astype(jnp.float32).reshape(count, rows, HEAD_DIM)
-        mixed = None
-        for which in range(4):
-            if which < 3:
-                value = plain + act[1, which, :, lanes][:, None, :]
-                value = value.reshape(tokens, HEAD_DIM).astype(jnp.bfloat16)
-            else:
-                value = rv[:, lanes]
+        plain = rv[:, head * patch : (head + 1) * patch].astype(jnp.float32)
+        plain = plain.reshape(count, rows, patch)
+        by_mouse, by_key = (
+            contract_last(act[1, which, :, lanes].astype(jnp.bfloat16), own_weight[:, lanes])
+            for which in (1, 2)
+        )
+        shifts = (by_key + by_mouse, by_mouse, by_key, None)
+        for which, shift in enumerate(shifts):
+            value = plain if shift is None else plain + shift[:, None, :]
+            value = value.reshape(tokens, patch).astype(jnp.bfloat16)
             summed = jnp.dot(wts[head * 4 + which], value, preferred_element_type=jnp.float32)
-            attended = (summed / totals[head * 4 + which]).astype(jnp.bfloat16)
-            term = guide_s[which] * attended.astype(jnp.float32)
-            mixed = term if mixed is None else mixed + term
-        combined.append(mixed.astype(jnp.bfloat16))
-    joined = jnp.concatenate(combined, axis=1).reshape(count, 2, half, cols)
-    blank = jnp.zeros(ow.shape, ow.dtype)
-    left_weight = jnp.concatenate([ow[...], blank], axis=0)
-    right_weight = jnp.concatenate([blank, ow[...]], axis=0)
-    part_sums = contract_last(
-        joined[:, 0].reshape(count * half, cols), left_weight
-    ) + contract_last(joined[:, 1].reshape(count * half, cols), right_weight)
-    psend[...] = part_sums.reshape(count, half, 2 * patch).astype(psend.dtype)
+            term = guide_s[which] * (summed / totals[head * 4 + which])
+            part_sums = term if part_sums is None else part_sums + term
+    split = part_sums.reshape(count, 2, half, patch)
+    psend[...] = jnp.concatenate([split[:, 0], split[:, 1]], axis=2).astype(psend.dtype)
 
     for step, peer in enumerate(peers):
         copy = pltpu.make_async_remote_copy(
@@ -717,10 +722,11 @@
             pltpu.VMEM((rows, width), bf16),
             pltpu.VMEM((tokens, cols), bf16),
             pltpu.VMEM((tokens, cols), bf16),
-            pltpu.VMEM((tokens, cols), bf16),
+            pltpu.VMEM((tokens, cols // HEAD_DIM * patch), bf16),
             pltpu.VMEM((key_table.shape[0], 2, cols), bf16),
             pltpu.VMEM((mouse_table.shape[0], 2, cols), bf16),
-            pltpu.VMEM((patch, cols), bf16),
+            pltpu.VMEM((patch, width), bf16),
+            pltpu.VMEM((count, rows, cols // HEAD_DIM * patch), bf16),
             pltpu.VMEM((rows, patch), f32),
             pltpu.VMEM((9 * lat_ch, dec), bf16),
             pltpu.VMEM((dec,), f32),

time: 27.5 us -> 26.8 us (0.975)
  Pallas kernels: 25.5 us -> 24.9 us
    pallas_call x1, Pallas kernels: 25.5 us -> 24.9 us  [fused_shards(): pl.pallas_call(functools.partial(fused, count), out_shape=(jax.ShapeDtype...]
where the time goes in v3:
time: 26.8 us; the launch traced here: 26.7 us
  Pallas kernels  24.9 us (93%)
  local copies, waits for them, and re-layouts  1.19 us (4%)
  between operations  0.64 us (2%)
    pallas_call x1, Pallas kernels, fused_shards(): pl.pallas_call(functools.partial(fused, count), out_shape=(jax.ShapeDtype...  24.9 us
    unnamed x2, local copies, waits for them, and re-layouts  1.19 us

profile of v3, /device:TPU:0, one launch (start us, length us, event | category | flops | bytes accessed | tf_op | source)
XLA Modules:
  0.0 26.7 jit_solution(17194869946001871525)
XLA Ops:
  0.6 24.9 %shard_map.140 = (f32[32,64]{1,0:T(8,128)S(1)}, f32[3,2,64]{2,1,0:T(2,128)S(1)}) custom-call(s32[8]{0:T(128)} %kb_hbm.1, s32[8]{0:T(128)} %ms_hbm.1, f32[4]{0:T(128)} %guide_hbm.1, bf16[32,4096]{1,0:T(8,128)(2,1)} %q_hbm.1, bf16[32,4096]{1,0:T(8,128)(2,1)} %k_hbm.1, bf16[32,4096]{1,0:T(8,128)(2,1)} %v_hbm.1, bf16[16,2,4096]{2,1,0:T(2,128)(2,1)} %kt_hbm.1, ...), custom_call_target="tpu_custom_call" | custom-call | tf_op jit(solution)/shard_map/pallas_call | solution.py:708
  25.5 0.6 %copy.17 = f32[32,64]{1,0:T(8,128)} copy(f32[32,64]{1,0:T(8,128)S(1)} %get-tuple-element.4) | data formatting | bytes 16384
  26.1 0.6 %copy.18 = f32[3,2,64]{2,1,0:T(2,128)} copy(f32[3,2,64]{2,1,0:T(2,128)S(1)} %get-tuple-element.5) | data formatting | bytes 3072
